TPU v7x, 512 devices: a whole 4x8x8 slice. The times are simulated.
512 devices in a mesh: row: 16 (over y_hi, x, core), col: 32 (over y_lo, z).
Axes of the slice: x: 4, y: 8 (y_hi: 2, y_lo: 4; y = y_hi * 4 + y_lo), z: 8, core: 2. Of those that a mesh axis runs over, the one named last changes fastest.
Arguments:
- covariance: float32 [8192, 8192], P('row', 'col'), may hold values from -8 to 8, as said below
- couplings: float32 [64, 9, 128, 128], P('row'), may hold values from -0.1875 to 0.1875
- block_columns: int32 [64, 9], replicated, may hold values from 0 to 63, as said below
- onsite: float32 [64], replicated, may hold values from 0.04 to 0.2
Outputs:
- new_covariance: float32 [8192, 8192], P('row', 'col')
Inputs may be any that keep to these rules, and one draw needn't show every extreme that they name: `block_columns`: each block row's 9 block columns are distinct and lie within 5 blocks of the row, counted cyclically over the 64 blocks; every row has one block column at distance 5 on each side. The covariance is skew-symmetric.
All inputs are finite; a program needn't handle non-finite values.
Results may differ from a plain program's by a relative error of at most 0.0001.
Values sent between devices are 32-bit elements; how exact they have to be, the bound alone decides.
A program may use at most 64 MiB of HBM per device.

v0:
```python
import jax
import jax.numpy as jnp
from jax import lax
from jax.sharding import PartitionSpec as P

BLOCK = 128
REACH = 5


step_size = 0.25


def from_root(block, axis, holder):
    block = jnp.where(lax.axis_index(axis) == holder, block, jnp.zeros_like(block))
    return lax.psum(block, axis)


def shifted(block, axis, distance):
    devices = range(lax.axis_size(axis))
    route = [((i - distance) % len(devices), i) for i in devices]
    return lax.ppermute(block, axis, route)


def relative_positions(columns, first_block, count, total_blocks):
    own_ids = first_block + jnp.arange(count, dtype=jnp.int32)
    relative = (columns - own_ids[:, None] + total_blocks // 2) % total_blocks - total_blocks // 2
    return jnp.arange(count, dtype=jnp.int32)[:, None] + relative + REACH


def on_device(covariance, couplings, block_columns, onsite):
    tile_rows, tile_cols = covariance.shape
    row_blocks = tile_rows // BLOCK
    col_blocks = tile_cols // BLOCK
    total_blocks = block_columns.shape[0]
    reach_cells = REACH * BLOCK
    row_hops = -(-reach_cells // tile_rows)
    col_hops = -(-reach_cells // tile_cols)
    first_row = lax.axis_index("row") * row_blocks
    first_col = lax.axis_index("col") * col_blocks
    own_offset = jnp.clip(first_col - first_row, 0, row_blocks - col_blocks)
    col_root = first_col // row_blocks
    own_couplings = lax.dynamic_slice_in_dim(couplings, own_offset, col_blocks, 0)
    col_couplings = from_root(own_couplings, "row", col_root)
    row_columns = lax.dynamic_slice_in_dim(block_columns, first_row, row_blocks, 0)
    col_columns = lax.dynamic_slice_in_dim(block_columns, first_col, col_blocks, 0)
    row_positions = relative_positions(row_columns, first_row, row_blocks, total_blocks)
    col_positions = relative_positions(col_columns, first_col, col_blocks, total_blocks)
    row_gains = lax.dynamic_slice_in_dim(onsite, first_row, row_blocks, 0)
    col_gains = lax.dynamic_slice_in_dim(onsite, first_col, col_blocks, 0)
    middle = 0.5 * (covariance + covariance)
    shaped = middle.reshape(row_blocks, BLOCK, col_blocks, BLOCK)
    picked = lax.dynamic_slice_in_dim(shaped, own_offset, col_blocks, 0)
    indices = jnp.arange(col_blocks, dtype=jnp.int32)
    local_diagonal = picked[indices, :, indices, :]
    received = []
    for root_part in range(row_blocks // col_blocks):
        received.append(from_root(local_diagonal, "col", first_row // col_blocks + root_part))
    row_diagonal = jnp.concatenate(received, axis=0)
    lower_parts = []
    upper_parts = []
    for distance in range(1, row_hops + 1):
        needed = min(tile_rows, reach_cells - (distance - 1) * tile_rows)
        from_lower = shifted(middle, "row", distance)
        from_upper = shifted(middle, "row", -distance)
        lower_parts.insert(0, from_lower[from_lower.shape[0] - needed :])
        upper_parts.append(from_upper[:needed])
    extended_rows = jnp.concatenate(lower_parts + [middle] + upper_parts, axis=0).reshape(
        -1, BLOCK, tile_cols
    )
    picked_rows = jnp.take(extended_rows, row_positions, axis=0)
    left_part = jnp.einsum(
        "ikab,ikbn->ian", couplings, picked_rows, precision=lax.Precision.HIGHEST
    )
    left_part = left_part + jnp.einsum(
        "iab,ibn->ian",
        row_diagonal * row_gains[:, None, None],
        middle.reshape(row_blocks, BLOCK, tile_cols),
        precision=lax.Precision.HIGHEST,
    )
    left_part = left_part.reshape(tile_rows, tile_cols)
    col_diagonal = from_root(local_diagonal, "row", col_root)
    left_parts = []
    right_parts = []
    for distance in range(1, col_hops + 1):
        needed = min(tile_cols, reach_cells - (distance - 1) * tile_cols)
        from_left = shifted(middle, "col", distance)
        from_right = shifted(middle, "col", -distance)
        left_parts.insert(0, from_left[:, from_left.shape[1] - needed :])
        right_parts.append(from_right[:, :needed])
    extended_cols = jnp.concatenate(left_parts + [middle] + right_parts, axis=1).reshape(
        tile_rows, -1, BLOCK
    )
    picked_cols = jnp.take(extended_cols, col_positions, axis=1)
    right_part = jnp.einsum(
        "nikb,ikab->nia", picked_cols, col_couplings, precision=lax.Precision.HIGHEST
    )
    right_part = right_part + jnp.einsum(
        "nib,iab->nia",
        middle.reshape(tile_rows, col_blocks, BLOCK),
        col_diagonal * col_gains[:, None, None],
        precision=lax.Precision.HIGHEST,
    )
    right_part = right_part.reshape(tile_rows, tile_cols)
    return covariance + step_size * (left_part + right_part)


def solution(mesh):
    return jax.shard_map(
        on_device,
        mesh=mesh,
        in_specs=(P("row", "col"), P("row", None, None, None), P(), P()),
        out_specs=P("row", "col"),
        check_vma=False,
    )
```

profile of v0, /device:TPU:22, one launch (start us, length us, event | category | flops | bytes accessed | tf_op | source)
XLA Modules:
  0.0 611.3 jit_solution(17752457273522759760)
XLA Ops:
  6.6 2.0 add_multiply_fusion
  8.6 1.3 reshape.42
  11.4 7.9 %collective-permute-start.4 = (f32[512,256]{1,0:T(8,128)}, f32[512,256]{1,0:T(8,128)}, u32[]{:S(2)}, u32[]{:S(2)}) collective-permute-start(f32[512,256]{1,0:T(8,128)} %add_multiply_fusion), channel_id=1, source_target_pairs={{29,0},{30,1},{31,2},{0,3},{1,4},{2,5},{3,6},{4,7},{5,8},{6,9},{7,... | collective-permute-start | bytes 1572872 | tf_op jit(solution)/shard_map/ppermute | solution.py:21
  19.3 6.4 %collective-permute-start.5 = (f32[512,256]{1,0:T(8,128)}, f32[512,256]{1,0:T(8,128)}, u32[]{:S(2)}, u32[]{:S(2)}) collective-permute-start(f32[512,256]{1,0:T(8,128)} %add_multiply_fusion), channel_id=1, source_target_pairs={{30,0},{31,1},{0,2},{1,3},{2,4},{3,5},{4,6},{5,7},{6,8},{7,9},{8,1... | collective-permute-start | bytes 1572872 | tf_op jit(solution)/shard_map/ppermute | solution.py:21
  25.7 3.4 collective-permute-start.6
  29.1 5.9 collective-permute-start
  35.0 1.9 collective-permute-start.1
  39.0 25.1 %collective-permute-done = f32[512,256]{1,0:T(8,128)} collective-permute-done((f32[512,256]{1,0:T(8,128)}, f32[512,256]{1,0:T(8,128)}, u32[]{:S(2)}, u32[]{:S(2)}) %collective-permute-start) | collective-permute-done | bytes 524320 | tf_op jit(solution)/shard_map/ppermute | solution.py:21
  64.2 1.9 collective-permute-start.7
  66.1 1.6 slice_dynamic-update-slice_fusion.3
  67.6 14.9 %collective-permute-done.4 = f32[512,256]{1,0:T(8,128)} collective-permute-done((f32[512,256]{1,0:T(8,128)}, f32[512,256]{1,0:T(8,128)}, u32[]{:S(2)}, u32[]{:S(2)}) %collective-permute-start.4) | collective-permute-done | bytes 524320 | tf_op jit(solution)/shard_map/ppermute | solution.py:21
  82.5 1.9 collective-permute-start.8
  84.4 1.7 slice_dynamic-update-slice_fusion.1
  86.1 2.4 collective-permute-start.9
  88.5 2.0 constant_dynamic-update-slice_fusion.7
  90.5 12.5 %collective-permute-done.6 = f32[512,256]{1,0:T(8,128)S(1)} collective-permute-done((f32[512,256]{1,0:T(8,128)}, f32[512,256]{1,0:T(8,128)S(1)}, u32[]{:S(2)}, u32[]{:S(2)}) %collective-permute-start.6) | collective-permute-done | bytes 524320 | tf_op jit(solution)/shard_map/ppermute | solution.py:21
  103.0 1.9 collective-permute-start.2
  105.9 1.9 collective-permute-start.3
  108.6 1.3 constant_dynamic-update-slice_fusion.1
  110.8 12.7 %collective-permute-done.8 = f32[512,256]{1,0:T(8,128)S(1)} collective-permute-done((f32[512,256]{1,0:T(8,128)}, f32[512,256]{1,0:T(8,128)S(1)}, u32[]{:S(2)}, u32[]{:S(2)}) %collective-permute-start.8) | collective-permute-done | bytes 524320 | tf_op jit(solution)/shard_map/ppermute | solution.py:21
  124.5 12.2 %collective-permute-done.9 = f32[512,256]{1,0:T(8,128)S(1)} collective-permute-done((f32[512,256]{1,0:T(8,128)}, f32[512,256]{1,0:T(8,128)S(1)}, u32[]{:S(2)}, u32[]{:S(2)}) %collective-permute-start.9) | collective-permute-done | bytes 524320 | tf_op jit(solution)/shard_map/ppermute | solution.py:21
  137.5 3.6 copy.35
  141.1 2.4 copy.36
  143.5 3.0 gather_fusion.2
  146.5 1.9 constant_dynamic-update-slice_fusion
  148.3 1.6 slice_dynamic-update-slice_fusion.2
  149.9 4.7 gather_fusion
  154.6 5.4 fusion.9
  160.0 235.1 %all-reduce.5.cloned.1.call-done = (f32[2,128,128]{2,1,0:T(8,128)}, f32[2,128,128]{2,1,0:T(8,128)}) async-done(((f32[2,128,128]{2,1,0:T(8,128)}, f32[2,128,128]{2,1,0:T(8,128)}), (f32[2,128,128]{2,1,0:T(8,128)}, f32[2,128,128]{2,1,0:T(8,128)})) %all-reduce.5.cloned.1.call-update) | async-done | bytes 262160 | tf_op jit(solution)/shard_map/psum | solution.py:15
  395.1 1.8 convolution_add_fusion.1
  396.9 198.1 %all-reduce.7.cloned.1.call-done = (f32[2,9,128,128]{3,2,1,0:T(8,128)}, f32[2,128,128]{2,1,0:T(8,128)}) async-done(((f32[2,9,128,128]{3,2,1,0:T(8,128)}, f32[2,128,128]{2,1,0:T(8,128)}), (f32[2,9,128,128]{3,2,1,0:T(8,128)}, f32[2,128,128]{2,1,0:T(8,128)})) %all-reduce.7.cloned.1.call-update) | async-done | bytes 1310736 | tf_op jit(solution)/shard_map/psum | solution.py:15
  595.0 7.7 %fusion.12 = f32[2,128,512]{2,1,0:T(8,128)S(1)} fusion(f32[2,9,128,128]{3,2,1,0:T(8,128)} %get-tuple-element.7, f32[2,9,512,128]{3,2,1,0:T(8,128)} %bitcast.37, pred[2,9]{1,0:T(4,128)(4,1)S(1)} %get-tuple-element.11), kind=kOutput, calls=%fused_computation.13 | convolution fusion | flops 1813118976 | bytes 6422546 | tf_op jit(solution)/shard_map/nikb,ikab->nia/dot_general | solution.py:94
  (53 shorter events, 9.6 us)
Async XLA Ops:
  6.5 31.6 %copy-start = (s32[64,9]{0,1:T(8,128)S(1)}, s32[64,9]{0,1:T(8,128)}, u32[]{:S(2)}) copy-start(s32[64,9]{0,1:T(8,128)} %param.6) | copy-start | bytes 6916
  6.5 30.4 %copy-start.1 = (f32[4,9,128,128]{3,2,1,0:T(8,128)S(1)}, f32[4,9,128,128]{3,2,1,0:T(8,128)}, u32[]{:S(2)}) copy-start(f32[4,9,128,128]{3,2,1,0:T(8,128)} %param.5) | copy-start | bytes 7077892
  6.5 388.6 %all-reduce.5.cloned.1.call-start = ((), (), s32[]{:S(2)}) async-start(), calls=%async_computation | async-start | bytes 524288 | tf_op jit(solution)/shard_map/psum | solution.py:15
  9.9 28.9 %copy-start.7 = (f32[64]{0:T(128)S(1)}, f32[64]{0:T(128)}, u32[]{:S(2)}) copy-start(f32[64]{0:T(128)} %param.7) | copy-start | bytes 772
  11.4 583.7 %all-reduce.7.cloned.1.call-start = ((), (), s32[]{:S(2)}) async-start(), calls=%async_computation.1 | async-start | bytes 2621440 | tf_op jit(solution)/shard_map/psum | solution.py:15
  11.4 71.1 %collective-permute-start.4 = (f32[512,256]{1,0:T(8,128)}, f32[512,256]{1,0:T(8,128)}, u32[]{:S(2)}, u32[]{:S(2)}) collective-permute-start(f32[512,256]{1,0:T(8,128)} %add_multiply_fusion), channel_id=1, source_target_pairs={{29,0},{30,1},{31,2},{0,3},{1,4},{2,5},{3,6},{4,7},{5,8},{6,9},{7,... | collective-permute-start | bytes 1572872 | tf_op jit(solution)/shard_map/ppermute | solution.py:21
  19.3 66.8 %collective-permute-start.5 = (f32[512,256]{1,0:T(8,128)}, f32[512,256]{1,0:T(8,128)}, u32[]{:S(2)}, u32[]{:S(2)}) collective-permute-start(f32[512,256]{1,0:T(8,128)} %add_multiply_fusion), channel_id=1, source_target_pairs={{30,0},{31,1},{0,2},{1,3},{2,4},{3,5},{4,6},{5,7},{6,8},{7,9},{8,1... | collective-permute-start | bytes 1572872 | tf_op jit(solution)/shard_map/ppermute | solution.py:21
  25.7 77.3 %collective-permute-start.6 = (f32[512,256]{1,0:T(8,128)}, f32[512,256]{1,0:T(8,128)S(1)}, u32[]{:S(2)}, u32[]{:S(2)}) collective-permute-start(f32[512,256]{1,0:T(8,128)} %add_multiply_fusion), channel_id=1, source_target_pairs={{31,0},{0,1},{1,2},{2,3},{3,4},{4,5},{5,6},{6,7},{7,8},{8,9},{9,10... | collective-permute-start | bytes 1572872 | tf_op jit(solution)/shard_map/ppermute | solution.py:21
  29.1 35.0 %collective-permute-start = (f32[512,256]{1,0:T(8,128)}, f32[512,256]{1,0:T(8,128)}, u32[]{:S(2)}, u32[]{:S(2)}) collective-permute-start(f32[512,256]{1,0:T(8,128)} %add_multiply_fusion), channel_id=1, source_target_pairs={{448,0},{480,32},{0,64},{32,96},{64,128},{96,160},{128,192},{160,2... | collective-permute-start | bytes 1572872 | tf_op jit(solution)/shard_map/ppermute | solution.py:21
  35.0 70.9 %collective-permute-start.1 = (f32[512,256]{1,0:T(8,128)}, f32[512,256]{1,0:T(8,128)S(1)}, u32[]{:S(2)}, u32[]{:S(2)}) collective-permute-start(f32[512,256]{1,0:T(8,128)} %add_multiply_fusion), channel_id=1, source_target_pairs={{480,0},{0,32},{32,64},{64,96},{96,128},{128,160},{160,192},{192,2... | collective-permute-start | bytes 1572872 | tf_op jit(solution)/shard_map/ppermute | solution.py:21
  38.1 70.5 %copy-start.3 = (f32[512,256]{1,0:T(8,128)S(1)}, f32[512,256]{1,0:T(8,128)}, u32[]{:S(2)}) copy-start(f32[512,256]{1,0:T(8,128)} %param.4) | copy-start | bytes 1572868
  64.2 45.8 %collective-permute-start.7 = (f32[512,256]{1,0:T(8,128)}, f32[512,256]{1,0:T(8,128)S(1)}, u32[]{:S(2)}, u32[]{:S(2)}) collective-permute-start(f32[512,256]{1,0:T(8,128)} %add_multiply_fusion), channel_id=1, source_target_pairs={{1,0},{2,1},{3,2},{4,3},{5,4},{6,5},{7,6},{8,7},{9,8},{10,9},{11,1... | collective-permute-start | bytes 1572872 | tf_op jit(solution)/shard_map/ppermute | solution.py:21
  82.5 41.1 %collective-permute-start.8 = (f32[512,256]{1,0:T(8,128)}, f32[512,256]{1,0:T(8,128)S(1)}, u32[]{:S(2)}, u32[]{:S(2)}) collective-permute-start(f32[512,256]{1,0:T(8,128)} %add_multiply_fusion), channel_id=1, source_target_pairs={{2,0},{3,1},{4,2},{5,3},{6,4},{7,5},{8,6},{9,7},{10,8},{11,9},{12,... | collective-permute-start | bytes 1572872 | tf_op jit(solution)/shard_map/ppermute | solution.py:21
  86.1 50.6 %collective-permute-start.9 = (f32[512,256]{1,0:T(8,128)}, f32[512,256]{1,0:T(8,128)S(1)}, u32[]{:S(2)}, u32[]{:S(2)}) collective-permute-start(f32[512,256]{1,0:T(8,128)} %add_multiply_fusion), channel_id=1, source_target_pairs={{3,0},{4,1},{5,2},{6,3},{7,4},{8,5},{9,6},{10,7},{11,8},{12,9},{13... | collective-permute-start | bytes 1572872 | tf_op jit(solution)/shard_map/ppermute | solution.py:21
  103.0 43.4 %collective-permute-start.2 = (f32[512,256]{1,0:T(8,128)}, f32[512,256]{1,0:T(8,128)}, u32[]{:S(2)}, u32[]{:S(2)}) collective-permute-start(f32[512,256]{1,0:T(8,128)} %add_multiply_fusion), channel_id=1, source_target_pairs={{32,0},{64,32},{96,64},{128,96},{160,128},{192,160},{224,192},{256... | collective-permute-start | bytes 1572872 | tf_op jit(solution)/shard_map/ppermute | solution.py:21
  105.9 42.5 %collective-permute-start.3 = (f32[512,256]{1,0:T(8,128)}, f32[512,256]{1,0:T(8,128)}, u32[]{:S(2)}, u32[]{:S(2)}) collective-permute-start(f32[512,256]{1,0:T(8,128)} %add_multiply_fusion), channel_id=1, source_target_pairs={{64,0},{96,32},{128,64},{160,96},{192,128},{224,160},{256,192},{28... | collective-permute-start | bytes 1572872 | tf_op jit(solution)/shard_map/ppermute | solution.py:21
  149.9 4.7 copy-start.2
  595.0 7.7 %copy-start.5 = (f32[64,2,8,128]{3,2,1,0:T(8,128)S(1)}, f32[64,2,8,128]{3,2,1,0:T(8,128)}, u32[]{:S(2)}) copy-start(f32[64,2,8,128]{3,2,1,0:T(8,128)} %get-tuple-element.15) | copy-start | bytes 1572868
  595.0 7.7 %copy-start.6 = (f32[2,128,128]{2,1,0:T(8,128)S(1)}, f32[2,128,128]{2,1,0:T(8,128)}, u32[]{:S(2)}) copy-start(f32[2,128,128]{2,1,0:T(8,128)} %get-tuple-element.8) | copy-start | bytes 393220
  595.0 8.5 %copy-start.4 = (f32[512,256]{1,0:T(8,128)S(1)}, f32[512,256]{1,0:T(8,128)}, u32[]{:S(2)}) copy-start(f32[512,256]{1,0:T(8,128)} %param.4) | copy-start | bytes 1572868
Sparse Core Ops, SparseCore 0:
  11.5 383.5 all-reduce.4
  398.1 196.8 all-reduce.6
where the time goes:
time: 617 us; the launch traced here: 611 us
  waiting for transfers between devices  511 us (83%)
  starting transfers between devices  35.6 us (6%)
  local copies, waits for them, and re-layouts  29.4 us (5%)
  matrix products  15.5 us (3%)
  between operations  13.7 us (2%)
  other arithmetic  6.41 us (1%)
    psum x2, waiting for transfers between devices, from_root(): return lax.psum(block, axis)  433 us
    ppermute x10, waiting for transfers between devices, shifted(): return lax.ppermute(block, axis, route)  77.5 us
    ppermute x10, starting transfers between devices, shifted(): return lax.ppermute(block, axis, route)  35.5 us
  transfers between devices with their start and end apart: 12, of which 7 were waited for; matrix products, arithmetic and copies ran while one was open for 6% of the time, Pallas kernels for 0%

commit v1 on v0

v1 whole, which is shorter than its diff:
```python
import functools

import jax
import jax.numpy as jnp
from jax import lax
from jax.experimental import pallas as pl
from jax.experimental.pallas import tpu as pltpu
from jax.sharding import PartitionSpec as P

MESH = pl.DeviceIdType.MESH
BLOCK = 128
REACH = 5
ROWB = 4
COLB = 2
BAND = 2 * REACH + 1
EXT = ROWB + 2 * REACH
STEP = 0.25
ZN = 8
YN = 4


def kernel(
    nrow, nb, nnz,
    cov, coup, cols, onsite, out,
    ext, cbuf, dbuf, ehi, elo, hs, lbuf, tbuf,
    load_sem, hsend, hrecv, dsend1, dsend2, drecv, tsend, trecv,
):
    r = lax.axis_index("row")
    c = lax.axis_index("col")
    zz = lax.rem(c, ZN)
    yy = c // ZN
    tr = ROWB * BLOCK

    def rowdev(d):
        return lax.rem(r + d + nrow, nrow), c

    def zdev(k):
        return r, yy * ZN + lax.rem(zz + k, ZN)

    def ydev(k):
        return r, lax.rem(yy + k, YN) * ZN + zz

    mirror = [(c // 2, 2 * r + h) for h in range(2)]
    side = lax.rem(c, 2)
    on_diag = r == c // 2

    barrier = pltpu.get_barrier_semaphore()
    near = [rowdev(d) for d in (-2, -1, 1, 2)]
    near += [zdev(k) for k in range(1, ZN)] + [ydev(k) for k in range(1, YN)]
    for dev in near:
        pl.semaphore_signal(barrier, inc=1, device_id=dev, device_id_type=MESH)
    for h in range(2):
        @pl.when(jnp.logical_not(jnp.logical_and(on_diag, side == h)))
        def _():
            pl.semaphore_signal(barrier, inc=1, device_id=mirror[h], device_id_type=MESH)

    own = pltpu.make_async_copy(cov, ext.at[pl.ds(REACH * BLOCK, tr)], load_sem.at[0])
    own.start()
    load_c = pltpu.make_async_copy(coup, cbuf.at[:, pl.ds(0, nnz)], load_sem.at[1])
    load_c.start()
    cbuf[:, nnz] = jnp.zeros((ROWB, BLOCK, BLOCK), jnp.float32)

    pl.semaphore_wait(barrier, len(near) + 2 - on_diag.astype(jnp.int32))

    halo = []
    plan = [
        (1, 0, tr, BLOCK),
        (-1, 0, tr, (REACH + ROWB) * BLOCK),
        (2, tr - BLOCK, BLOCK, 0),
        (-2, 0, BLOCK, (EXT - 1) * BLOCK),
    ]
    for n, (d, start, size, dst) in enumerate(plan):
        cp = pltpu.make_async_remote_copy(
            src_ref=cov.at[pl.ds(start, size)],
            dst_ref=ext.at[pl.ds(dst, size)],
            send_sem=hsend.at[n], recv_sem=hrecv.at[n],
            device_id=rowdev(d), device_id_type=MESH,
        )
        cp.start()
        halo.append(cp)

    def z_sends(g):
        return [
            pltpu.make_async_remote_copy(
                src_ref=dbuf.at[pl.ds(2 * g, 2)], dst_ref=dbuf.at[pl.ds(2 * g, 2)],
                send_sem=dsend2.at[k - 1], recv_sem=drecv.at[g],
                device_id=zdev(k), device_id_type=MESH,
            )
            for k in range(1, ZN)
        ]

    def y_sends(g):
        return [
            pltpu.make_async_remote_copy(
                src_ref=dbuf.at[pl.ds(2 * g, 2)], dst_ref=dbuf.at[pl.ds(2 * g, 2)],
                send_sem=dsend1.at[k - 1], recv_sem=drecv.at[g],
                device_id=ydev(k), device_id_type=MESH,
            )
            for k in range(1, YN)
        ]

    own_y = yy == r // 4
    for g in range(2):
        is_z = zz == lax.rem(2 * r + g, ZN)
        is_root = jnp.logical_and(is_z, own_y)

        @pl.when(is_root)
        def _():
            copies = []
            for b in range(2):
                cp = pltpu.make_async_copy(
                    cov.at[pl.ds((2 * g + b) * BLOCK, BLOCK), pl.ds(b * BLOCK, BLOCK)],
                    dbuf.at[2 * g + b], load_sem.at[2 + b],
                )
                cp.start()
                copies.append(cp)
            for cp in copies:
                cp.wait()
            for cp in y_sends(g) + z_sends(g):
                cp.start()

    load_c.wait()
    own.wait()

    def split(v):
        hi = v.astype(jnp.bfloat16)
        return hi, (v - hi.astype(jnp.float32)).astype(jnp.bfloat16)

    def put_h(i, t, v):
        hi, lo = split(v)
        hs[pl.ds(i * BLOCK, BLOCK), pl.ds(t * BLOCK, BLOCK)] = hi
        hs[pl.ds(tr + i * BLOCK, BLOCK), pl.ds(t * BLOCK, BLOCK)] = lo

    centre = []
    for i in range(ROWB):
        row = ROWB * r + i
        slots = [
            jnp.bitwise_and(cols[row, k] - row + nb // 2, nb - 1) - nb // 2 + REACH
            for k in range(nnz)
        ]
        for o in range(BAND):
            which = jnp.int32(nnz)
            for k in range(nnz):
                which = jnp.where(slots[k] == o, k, which)
            if o == REACH:
                centre.append(which)
            else:
                put_h(i, i + o, cbuf[i, which])
        for t in range(EXT):
            if t < i or t > i + BAND - 1:
                zero = jnp.zeros((BLOCK, BLOCK), jnp.bfloat16)
                hs[pl.ds(i * BLOCK, BLOCK), pl.ds(t * BLOCK, BLOCK)] = zero
                hs[pl.ds(tr + i * BLOCK, BLOCK), pl.ds(t * BLOCK, BLOCK)] = zero

    def put_e(start, size):
        hi, lo = split(ext[pl.ds(start, size)])
        ehi[pl.ds(start, size)] = hi
        elo[pl.ds(start, size)] = lo

    put_e(REACH * BLOCK, tr)

    for g in range(2):
        is_z = zz == lax.rem(2 * r + g, ZN)
        is_root = jnp.logical_and(is_z, own_y)

        @pl.when(jnp.logical_not(is_root))
        def _():
            z_sends(g)[0].wait_recv()

        @pl.when(jnp.logical_and(is_z, jnp.logical_not(own_y)))
        def _():
            for cp in z_sends(g):
                cp.start()

    for i in range(ROWB):
        put_h(i, i + REACH, cbuf[i, centre[i]] + onsite[ROWB * r + i] * dbuf[i])

    for cp in halo:
        cp.wait_recv()
    put_e(0, REACH * BLOCK)
    put_e((REACH + ROWB) * BLOCK, REACH * BLOCK)

    both = jnp.dot(hs[...], ehi[...], preferred_element_type=jnp.float32)
    low = jnp.dot(hs[pl.ds(0, tr)], elo[...], preferred_element_type=jnp.float32)
    lbuf[...] = both[:tr] + both[tr:] + low

    def swap(i):
        h, b = i // 2, i % 2
        return pltpu.make_async_remote_copy(
            src_ref=lbuf.at[pl.ds(i * BLOCK, BLOCK)], dst_ref=tbuf.at[side, b],
            send_sem=tsend.at[i], recv_sem=trecv.at[side, b],
            device_id=mirror[h], device_id_type=MESH,
        )

    def keep(i):
        return pltpu.make_async_copy(
            lbuf.at[pl.ds(i * BLOCK, BLOCK)], tbuf.at[side, i % 2], trecv.at[side, i % 2]
        )

    for i in range(ROWB):
        mine = jnp.logical_and(on_diag, side == i // 2)

        @pl.when(mine)
        def _():
            keep(i).start()

        @pl.when(jnp.logical_not(mine))
        def _():
            swap(i).start()

    for g in range(2):
        for b in range(2):
            mine = jnp.logical_and(on_diag, side == g)

            @pl.when(mine)
            def _():
                pltpu.make_async_copy(
                    lbuf.at[pl.ds((2 * g + b) * BLOCK, BLOCK)], tbuf.at[g, b], trecv.at[g, b]
                ).wait()

            @pl.when(jnp.logical_not(mine))
            def _():
                pltpu.make_async_remote_copy(
                    src_ref=lbuf.at[pl.ds(0, BLOCK)], dst_ref=tbuf.at[g, b],
                    send_sem=tsend.at[0], recv_sem=trecv.at[g, b],
                    device_id=mirror[g], device_id_type=MESH,
                ).wait_recv()

            rows = pl.ds(g * 2 * BLOCK, 2 * BLOCK)
            lanes = pl.ds(b * BLOCK, BLOCK)
            here = ext[pl.ds((REACH + 2 * g) * BLOCK, 2 * BLOCK), lanes]
            out[rows, lanes] = here + STEP * (lbuf[rows, lanes] - tbuf[g, b].T)

    for cp in halo:
        cp.wait_send()
    for g in range(2):
        is_z = zz == lax.rem(2 * r + g, ZN)

        @pl.when(jnp.logical_and(is_z, own_y))
        def _():
            for cp in y_sends(g):
                cp.wait_send()

        @pl.when(is_z)
        def _():
            for cp in z_sends(g):
                cp.wait_send()
    for i in range(ROWB):
        @pl.when(jnp.logical_not(jnp.logical_and(on_diag, side == i // 2)))
        def _():
            swap(i).wait_send()


def solution(mesh):
    nrow = mesh.shape["row"]

    def on_device(covariance, couplings, block_columns, onsite):
        rows, width = covariance.shape
        nb, nnz = block_columns.shape
        f32, bf16 = jnp.float32, jnp.bfloat16
        dma = pltpu.SemaphoreType.DMA
        return pl.pallas_call(
            functools.partial(kernel, nrow, nb, nnz),
            out_shape=jax.ShapeDtypeStruct((rows, width), f32),
            in_specs=[
                pl.BlockSpec(memory_space=pl.ANY),
                pl.BlockSpec(memory_space=pl.ANY),
                pl.BlockSpec(memory_space=pltpu.SMEM),
                pl.BlockSpec(memory_space=pltpu.SMEM),
            ],
            out_specs=pl.BlockSpec(memory_space=pltpu.VMEM),
            scratch_shapes=[
                pltpu.VMEM((EXT * BLOCK, width), f32),
                pltpu.VMEM((ROWB, nnz + 1, BLOCK, BLOCK), f32),
                pltpu.VMEM((ROWB, BLOCK, BLOCK), f32),
                pltpu.VMEM((EXT * BLOCK, width), bf16),
                pltpu.VMEM((EXT * BLOCK, width), bf16),
                pltpu.VMEM((2 * rows, EXT * BLOCK), bf16),
                pltpu.VMEM((rows, width), f32),
                pltpu.VMEM((2, 2, BLOCK, width), f32),
                dma((4,)), dma((4,)), dma((4,)), dma((YN - 1,)), dma((ZN - 1,)),
                dma((2,)), dma((4,)), dma((2, 2)),
            ],
            compiler_params=pltpu.CompilerParams(
                collective_id=0, has_side_effects=True, vmem_limit_bytes=48 * 2**20
            ),
        )(covariance, couplings, block_columns, onsite)

    return jax.shard_map(
        on_device,
        mesh=mesh,
        in_specs=(P("row", "col"), P("row", None, None, None), P(), P()),
        out_specs=P("row", "col"),
        check_vma=False,
    )
```

time: 617 us -> 111 us (0.18)
  the two profiles are of different devices: /device:TPU:22 before, /device:TPU:473 now
where the time goes in v1:
time: 111 us
  Pallas kernels  106 us (95%)
  local copies, waits for them, and re-layouts  4.94 us (4%)
    pallas_call x1, Pallas kernels, on_device(): pl.pallas_call(functools.partial(kernel, nrow, nb, nnz), out_shape=jax.Sh...  106 us
    unnamed x8, local copies, waits for them, and re-layouts  4.94 us

profile of v1, /device:TPU:473, one launch (start us, length us, event | category | flops | bytes accessed | tf_op | source)
XLA Modules:
  0.0 111.0 jit_solution(2253320913957484716)
XLA Ops:
  0.0 0.8 copy.5.cols
  0.8 0.0 copy-start
  0.8 1.7 %copy-done = f32[4,9,128,128]{3,2,1,0:T(8,128)S(1)} copy-done((f32[4,9,128,128]{3,2,1,0:T(8,128)S(1)}, f32[4,9,128,128]{3,2,1,0:T(8,128)}, u32[]{:S(2)}) %copy-start) | copy-done | bytes 2359320
  2.5 0.0 copy-start.1
  2.5 1.0 copy-done.1
  3.5 0.0 copy-start.2
  3.5 0.7 copy-done.2
  4.1 106.0 %shard_map.46 = f32[512,256]{1,0:T(8,128)S(1)} custom-call(f32[512,256]{1,0:T(8,128)S(1)} %copy-done.1, f32[4,9,128,128]{3,2,1,0:T(8,128)S(1)} %copy-done, s32[64,9]{1,0:T(8,128)S(1)} %copy.5.cols, f32[64]{0:T(128)S(1)} %copy-done.2), custom_call_target="tpu_custom_call" | custom-call | tf_op jit(solution)/shard_map/pallas_call | solution.py:262
  110.2 0.8 copy.7
Async XLA Ops:
  0.8 1.7 %copy-start = (f32[4,9,128,128]{3,2,1,0:T(8,128)S(1)}, f32[4,9,128,128]{3,2,1,0:T(8,128)}, u32[]{:S(2)}) copy-start(f32[4,9,128,128]{3,2,1,0:T(8,128)} %coup.1) | copy-start | bytes 7077892
  2.5 1.0 copy-start.1
  3.5 0.7 copy-start.2

commit v2 on v1

v2 whole, which is shorter than its diff:
```python
import functools

import jax
import jax.numpy as jnp
from jax import lax
from jax.experimental import pallas as pl
from jax.experimental.pallas import tpu as pltpu
from jax.sharding import PartitionSpec as P

MESH = pl.DeviceIdType.MESH
BLOCK = 128
REACH = 5
ROWB = 4
COLB = 2
BAND = 2 * REACH + 1
EXT = ROWB + 2 * REACH
STEP = 0.25
ZN = 8
i32 = jnp.int32


def both(a, b):
    return jnp.logical_and(a, b)


def kernel(
    nrow, nb, nnz,
    cov, coup, cols_h, onsite_h, out,
    cols, onsite, ext, cbuf, dbuf, dterm, ehi, elo, hs, lbuf, rbuf, tbuf,
    load_sem, hsend, hrecv, dsend, drecv, tsend, fsend, rrecv, trecv,
):
    r = lax.axis_index("row")
    c = lax.axis_index("col")
    zz = lax.rem(c, ZN)
    yy = c // ZN
    tr = ROWB * BLOCK
    half = 2 * BLOCK

    def rowdev(d):
        return lax.rem(r + d + nrow, nrow), c

    def is_me(dev):
        return both(dev[0] == r, dev[1] == c)

    def target(rs, cs, h):
        return cs // 2, 2 * rs + h

    def relay(rs, cs):
        return (
            (cs // 16) * 8 + lax.rem(cs // 4, 4) * 2 + lax.rem(rs, 2),
            (rs // 4) * ZN + lax.rem(cs, ZN),
        )

    direct = is_me(relay(r, c))
    sources = [
        ((c // 8) * 4 + 2 * s + lax.rem(r, 2), (r // 4) * ZN + zz) for s in range(2)
    ]
    is_relay = lax.rem(r // 2, 2) == zz // 4
    relays_for = [both(is_relay, jnp.logical_not(is_me(d))) for d in sources]

    loads = [
        pltpu.make_async_copy(coup, cbuf.at[:, pl.ds(0, nnz)], load_sem.at[0]),
        pltpu.make_async_copy(cols_h, cols, load_sem.at[1]),
        pltpu.make_async_copy(onsite_h, onsite, load_sem.at[2]),
    ] + [
        pltpu.make_async_copy(
            cov.at[:, pl.ds(j * BLOCK, BLOCK)], ext.at[j, pl.ds(REACH * BLOCK, tr)],
            load_sem.at[3 + j],
        )
        for j in range(COLB)
    ]
    for cp in loads:
        cp.start()

    barrier = pltpu.get_barrier_semaphore()

    def tell(dev):
        pl.semaphore_signal(barrier, inc=1, device_id=dev, device_id_type=MESH)

    near = [rowdev(d) for d in (-2, -1, 1, 2)]
    root = c // 2
    same_core = lax.rem(r, 2) == lax.rem(root, 2)
    same_x = lax.rem(r // 2, 4) == lax.rem(root // 2, 4)
    is_root = r == root
    hub = both(same_core, same_x)
    leaf = both(same_core, jnp.logical_not(same_x))
    peer = (lax.rem(r + 8, nrow), c)
    pair = (r + 1 - 2 * lax.rem(r, 2), c)
    xdevs = [((r // 8) * 8 + lax.rem(r + 2 * k, 8), c) for k in (1, 3, 2)]
    for dev in near:
        tell(dev)
    @pl.when(leaf)
    def _():
        tell(((r // 8) * 8 + lax.rem(root, 8), c))

    @pl.when(r == lax.rem(root + 8, nrow))
    def _():
        tell(peer)

    for s in range(2):
        @pl.when(relays_for[s])
        def _():
            tell(sources[s])
    for g in range(2):
        origin = (c // 2, 2 * r + g)
        sender = relay(*origin)

        @pl.when(jnp.logical_not(is_me(sender)))
        def _():
            tell(sender)
    expected = len(near) + jnp.where(direct, 0, 1).astype(i32)
    expected = expected + jnp.where(is_root, 1, 0).astype(i32) + jnp.where(hub, 3, 0).astype(i32)
    for h in range(2):
        go = both(direct, jnp.logical_not(is_me(target(r, c, h))))
        expected = expected + jnp.where(go, 1, 0).astype(i32)
        for s in range(2):
            go = both(relays_for[s], jnp.logical_not(is_me(target(*sources[s], h))))
            expected = expected + jnp.where(go, 1, 0).astype(i32)

    cbuf[:, nnz] = jnp.zeros((ROWB, BLOCK, BLOCK), jnp.float32)
    pl.semaphore_wait(barrier, expected)

    plan = [
        (1, 0, tr, BLOCK),
        (-1, 0, tr, (REACH + ROWB) * BLOCK),
        (2, tr - BLOCK, BLOCK, 0),
        (-2, 0, BLOCK, (EXT - 1) * BLOCK),
    ]
    halo = [
        [
            pltpu.make_async_remote_copy(
                src_ref=cov.at[pl.ds(start, size), pl.ds(j * BLOCK, BLOCK)],
                dst_ref=ext.at[j, pl.ds(dst, size)],
                send_sem=hsend.at[j, n], recv_sem=hrecv.at[j, n],
                device_id=rowdev(d), device_id_type=MESH,
            )
            for n, (d, start, size, dst) in enumerate(plan)
        ]
        for j in range(COLB)
    ]

    def fan(devs, first):
        return [
            pltpu.make_async_remote_copy(
                src_ref=dbuf, dst_ref=dbuf, send_sem=dsend.at[first + k], recv_sem=drecv,
                device_id=dev, device_id_type=MESH,
            )
            for k, dev in enumerate(devs)
        ]

    def forward(cond, devs, first, start):
        @pl.when(cond)
        def _():
            for cp in fan(devs, first):
                if start:
                    cp.start()
                else:
                    cp.wait_send()

    def forwards(start, at_root):
        at = is_root if at_root else jnp.logical_not(is_root)
        if at_root:
            forward(at, [peer], 4, start)
        forward(both(hub, at), xdevs, 1, start)
        forward(both(same_core, at), [pair], 0, start)

    first_diag = 2 * lax.rem(c, 2) * BLOCK

    @pl.when(is_root)
    def _():
        copies = [
            pltpu.make_async_copy(
                cov.at[pl.ds(first_diag + b * BLOCK, BLOCK), pl.ds(b * BLOCK, BLOCK)],
                dbuf.at[b], load_sem.at[5 + b],
            )
            for b in range(2)
        ]
        for cp in copies:
            cp.start()
        for cp in copies:
            cp.wait()

    forwards(True, True)

    for j in range(COLB):
        for cp in halo[j]:
            cp.start()

    for cp in loads:
        cp.wait()

    def split(v):
        hi = v.astype(jnp.bfloat16)
        return hi, (v - hi.astype(jnp.float32)).astype(jnp.bfloat16)

    def put_h(i, t, v):
        hi, lo = split(v)
        hs[pl.ds(i * BLOCK, BLOCK), pl.ds(t * BLOCK, BLOCK)] = hi
        hs[pl.ds(tr + i * BLOCK, BLOCK), pl.ds(t * BLOCK, BLOCK)] = lo

    def put_e(j, start, size):
        hi, lo = split(ext[j, pl.ds(start, size)])
        ehi[j, pl.ds(start, size)] = hi
        elo[j, pl.ds(start, size)] = lo

    for i in range(ROWB):
        row = ROWB * r + i
        slots = [
            jnp.bitwise_and(cols[row, k] - row + nb // 2, nb - 1) - nb // 2 + REACH
            for k in range(nnz)
        ]
        for o in range(BAND):
            which = jnp.int32(nnz)
            for k in range(nnz):
                which = jnp.where(slots[k] == o, k, which)
            put_h(i, i + o, cbuf[i, which])
        for t in range(EXT):
            if t < i or t > i + BAND - 1:
                zero = jnp.zeros((BLOCK, BLOCK), jnp.bfloat16)
                hs[pl.ds(i * BLOCK, BLOCK), pl.ds(t * BLOCK, BLOCK)] = zero
                hs[pl.ds(tr + i * BLOCK, BLOCK), pl.ds(t * BLOCK, BLOCK)] = zero

    for j in range(COLB):
        put_e(j, REACH * BLOCK, tr)

    @pl.when(jnp.logical_not(is_root))
    def _():
        fan([pair], 0)[0].wait_recv()

    forwards(True, False)

    def dot_t(a, b):
        return lax.dot_general(
            a, b, (((1,), (1,)), ((), ())), preferred_element_type=jnp.float32
        )

    mid = pl.ds(REACH * BLOCK, tr)
    for j in range(COLB):
        dhi, dlo = split(onsite[COLB * c + j] * dbuf[j])
        yhi = ehi[j, mid]
        dterm[j] = dot_t(yhi, dhi) + dot_t(yhi, dlo) + dot_t(elo[j, mid], dhi)

    def remote(src, dst, ssem, rsem, dev):
        return pltpu.make_async_remote_copy(
            src_ref=src, dst_ref=dst, send_sem=ssem, recv_sem=rsem,
            device_id=dev, device_id_type=MESH,
        )

    def deliver(src, rs, cs, h, j, ssem):
        side = lax.rem(cs, 2)
        dev = target(rs, cs, h)
        mine = is_me(dev)

        @pl.when(mine)
        def _():
            pltpu.make_async_copy(src, tbuf.at[side, j], trecv.at[side, j]).start()

        @pl.when(jnp.logical_not(mine))
        def _():
            remote(src, tbuf.at[side, j], ssem, trecv.at[side, j], dev).start()

    def drain(src, rs, cs, h, j, ssem):
        side = lax.rem(cs, 2)
        dev = target(rs, cs, h)

        @pl.when(jnp.logical_not(is_me(dev)))
        def _():
            remote(src, tbuf.at[side, j], ssem, trecv.at[side, j], dev).wait_send()

    my_slot = lax.rem(r // 2, 2)

    def chunk(h):
        return pl.ds(h * half, half)

    def to_relay(h, j):
        return remote(
            lbuf.at[j, chunk(h)], rbuf.at[my_slot, j, chunk(h)],
            tsend.at[h, j], rrecv.at[my_slot, h, j], relay(r, c),
        )

    for j in range(COLB):
        for cp in halo[j]:
            cp.wait_recv()
        put_e(j, 0, REACH * BLOCK)
        put_e(j, (REACH + ROWB) * BLOCK, REACH * BLOCK)
        p = jnp.dot(hs[...], ehi[j], preferred_element_type=jnp.float32)
        q = jnp.dot(hs[pl.ds(0, tr)], elo[j], preferred_element_type=jnp.float32)
        lbuf[j] = p[:tr] + p[tr:] + q + dterm[j]

        @pl.when(direct)
        def _():
            for h in range(2):
                deliver(lbuf.at[j, chunk(h)], r, c, h, j, tsend.at[h, j])

        @pl.when(jnp.logical_not(direct))
        def _():
            for h in range(2):
                to_relay(h, j).start()

        for s in range(2):
            @pl.when(relays_for[s])
            def _():
                for h in range(2):
                    src = rbuf.at[s, j, chunk(h)]
                    pltpu.make_async_copy(src, src, rrecv.at[s, h, j]).wait()
                    deliver(src, *sources[s], h, j, fsend.at[s, h, j])

    for j in range(COLB):
        for g in range(2):
            dst = tbuf.at[g, j]
            pltpu.make_async_copy(dst, dst, trecv.at[g, j]).wait()
            rows = pl.ds((2 * g + j) * BLOCK, BLOCK)
            here = pl.ds((REACH + 2 * g + j) * BLOCK, BLOCK)
            turned = tbuf[g, j].T
            for b in range(COLB):
                lanes = pl.ds(b * BLOCK, BLOCK)
                mine = lbuf[b, rows] - turned[:, b * BLOCK:(b + 1) * BLOCK]
                out[rows, lanes] = ext[b, here] + STEP * mine

    for j in range(COLB):
        for cp in halo[j]:
            cp.wait_send()
    forwards(False, True)
    forwards(False, False)
    for j in range(COLB):
        for h in range(2):
            @pl.when(direct)
            def _():
                drain(lbuf.at[j, chunk(h)], r, c, h, j, tsend.at[h, j])

            @pl.when(jnp.logical_not(direct))
            def _():
                to_relay(h, j).wait_send()

            for s in range(2):
                @pl.when(relays_for[s])
                def _():
                    drain(rbuf.at[s, j, chunk(h)], *sources[s], h, j, fsend.at[s, h, j])


def solution(mesh):
    nrow = mesh.shape["row"]

    def on_device(covariance, couplings, block_columns, onsite):
        rows, width = covariance.shape
        nb, nnz = block_columns.shape
        f32, bf16 = jnp.float32, jnp.bfloat16
        dma = pltpu.SemaphoreType.DMA
        return pl.pallas_call(
            functools.partial(kernel, nrow, nb, nnz),
            out_shape=jax.ShapeDtypeStruct((rows, width), f32),
            in_specs=[pl.BlockSpec(memory_space=pl.ANY)] * 4,
            out_specs=pl.BlockSpec(memory_space=pltpu.VMEM),
            scratch_shapes=[
                pltpu.SMEM((nb, nnz), jnp.int32),
                pltpu.SMEM((nb,), f32),
                pltpu.VMEM((COLB, EXT * BLOCK, BLOCK), f32),
                pltpu.VMEM((ROWB, nnz + 1, BLOCK, BLOCK), f32),
                pltpu.VMEM((COLB, BLOCK, BLOCK), f32),
                pltpu.VMEM((COLB, rows, BLOCK), f32),
                pltpu.VMEM((COLB, EXT * BLOCK, BLOCK), bf16),
                pltpu.VMEM((COLB, EXT * BLOCK, BLOCK), bf16),
                pltpu.VMEM((2 * rows, EXT * BLOCK), bf16),
                pltpu.VMEM((COLB, rows, BLOCK), f32),
                pltpu.VMEM((2, COLB, rows, BLOCK), f32),
                pltpu.VMEM((2, COLB, 2 * BLOCK, BLOCK), f32),
                dma((7,)), dma((COLB, 4)), dma((COLB, 4)), dma((5,)), dma(()),
                dma((2, COLB)), dma((2, 2, COLB)), dma((2, 2, COLB)), dma((2, COLB)),
            ],
            compiler_params=pltpu.CompilerParams(
                collective_id=0, has_side_effects=True, vmem_limit_bytes=48 * 2**20
            ),
        )(covariance, couplings, block_columns, onsite)

    return jax.shard_map(
        on_device,
        mesh=mesh,
        in_specs=(P("row", "col"), P("row", None, None, None), P(), P()),
        out_specs=P("row", "col"),
        check_vma=False,
    )
```

time: 111 us -> 77 us (0.69)
  the two profiles are of different devices: /device:TPU:473 before, /device:TPU:37 now
where the time goes in v2:
time: 77 us; the launch traced here: 76.8 us
  Pallas kernels  71.8 us (93%)
  local copies, waits for them, and re-layouts  4.94 us (6%)
    pallas_call x1, Pallas kernels, on_device(): pl.pallas_call(functools.partial(kernel, nrow, nb, nnz), out_shape=jax.Sh...  71.8 us
    unnamed x8, local copies, waits for them, and re-layouts  4.94 us

profile of v2, /device:TPU:37, one launch (start us, length us, event | category | flops | bytes accessed | tf_op | source)
XLA Modules:
  0.0 76.8 jit_solution(5503543386635463976)
XLA Ops:
  0.0 0.8 %copy.5.cols_h = s32[64,9]{1,0:T(8,128)S(1)} copy(s32[64,9]{0,1:T(8,128)} %param.6) | data formatting | bytes 4608 | tf_op args[2]
  0.8 0.0 copy-start
  0.8 1.7 %copy-done = f32[4,9,128,128]{3,2,1,0:T(8,128)S(1)} copy-done((f32[4,9,128,128]{3,2,1,0:T(8,128)S(1)}, f32[4,9,128,128]{3,2,1,0:T(8,128)}, u32[]{:S(2)}) %copy-start) | copy-done | bytes 2359320
  2.5 0.0 copy-start.1
  2.5 1.0 %copy-done.1 = f32[512,256]{1,0:T(8,128)S(1)} copy-done((f32[512,256]{1,0:T(8,128)S(1)}, f32[512,256]{1,0:T(8,128)}, u32[]{:S(2)}) %copy-start.1) | copy-done | bytes 524312
  3.5 0.0 copy-start.2
  3.5 0.7 copy-done.2
  4.1 71.8 %shard_map.46 = f32[512,256]{1,0:T(8,128)S(1)} custom-call(f32[512,256]{1,0:T(8,128)S(1)} %copy-done.1, f32[4,9,128,128]{3,2,1,0:T(8,128)S(1)} %copy-done, s32[64,9]{1,0:T(8,128)S(1)} %copy.5.cols_h, f32[64]{0:T(128)S(1)} %copy-done.2), custom_call_target="tpu_custom_call" | custom-call | tf_op jit(solution)/shard_map/pallas_call | solution.py:349
  76.0 0.8 %copy.7 = f32[512,256]{1,0:T(8,128)} copy(f32[512,256]{1,0:T(8,128)S(1)} %shard_map.46) | data formatting | bytes 1048576
Async XLA Ops:
  0.8 1.7 %copy-start = (f32[4,9,128,128]{3,2,1,0:T(8,128)S(1)}, f32[4,9,128,128]{3,2,1,0:T(8,128)}, u32[]{:S(2)}) copy-start(f32[4,9,128,128]{3,2,1,0:T(8,128)} %coup.1) | copy-start | bytes 7077892
  2.5 1.0 %copy-start.1 = (f32[512,256]{1,0:T(8,128)S(1)}, f32[512,256]{1,0:T(8,128)}, u32[]{:S(2)}) copy-start(f32[512,256]{1,0:T(8,128)} %cov.1) | copy-start | bytes 1572868
  3.5 0.7 copy-start.2

commit v3 on v2

--- a/solution.py
+++ b/solution.py
@@ -45,18 +45,40 @@
     def target(rs, cs, h):
         return cs // 2, 2 * rs + h
 
-    def relay(rs, cs):
+    def same(a, b):
+        return both(a[0] == b[0], a[1] == b[1])
+
+    def part(k, cs):
+        return lax.rem(cs + 1 - k, 2)
+
+    def relay(k, rs, cs):
+        if k == 0:
+            return (
+                (cs // 16) * 8 + lax.rem(cs // 4, 4) * 2 + lax.rem(rs, 2),
+                (rs // 4) * ZN + lax.rem(cs, ZN),
+            )
         return (
-            (cs // 16) * 8 + lax.rem(cs // 4, 4) * 2 + lax.rem(rs, 2),
-            (rs // 4) * ZN + lax.rem(cs, ZN),
+            (rs // 8) * 8 + lax.rem(cs // 2, 8),
+            (cs // ZN) * ZN + lax.rem(2 * rs + part(k, cs), ZN),
         )
 
-    direct = is_me(relay(r, c))
+    def goal(k, rs, cs):
+        return target(rs, cs, part(k, cs))
+
+    def is_direct(k, rs, cs):
+        via = relay(k, rs, cs)
+        return jnp.logical_or(same(via, (rs, cs)), same(via, goal(k, rs, cs)))
+
+    direct = [is_direct(k, r, c) for k in range(2)]
     sources = [
-        ((c // 8) * 4 + 2 * s + lax.rem(r, 2), (r // 4) * ZN + zz) for s in range(2)
+        [((c // 8) * 4 + 2 * s + lax.rem(r, 2), (r // 4) * ZN + zz) for s in range(2)],
+        [((r // 8) * 8 + 4 * s + zz // 2, yy * ZN + lax.rem(r, 4) * 2 + lax.rem(c, 2)) for s in range(2)],
     ]
-    is_relay = lax.rem(r // 2, 2) == zz // 4
-    relays_for = [both(is_relay, jnp.logical_not(is_me(d))) for d in sources]
+    at_relay = [lax.rem(r // 2, 2) == zz // 4, lax.rem(r // 4, 2) == lax.rem(yy, 2)]
+    serves = [
+        [both(at_relay[k], jnp.logical_not(is_direct(k, *sources[k][s]))) for s in range(2)]
+        for k in range(2)
+    ]
 
     loads = [
         pltpu.make_async_copy(coup, cbuf.at[:, pl.ds(0, nnz)], load_sem.at[0]),
@@ -97,25 +119,33 @@
     def _():
         tell(peer)
 
-    for s in range(2):
-        @pl.when(relays_for[s])
-        def _():
-            tell(sources[s])
+    for k in range(2):
+        for s in range(2):
+            @pl.when(serves[k][s])
+            def _():
+                tell(sources[k][s])
     for g in range(2):
         origin = (c // 2, 2 * r + g)
-        sender = relay(*origin)
-
-        @pl.when(jnp.logical_not(is_me(sender)))
-        def _():
-            tell(sender)
-    expected = len(near) + jnp.where(direct, 0, 1).astype(i32)
-    expected = expected + jnp.where(is_root, 1, 0).astype(i32) + jnp.where(hub, 3, 0).astype(i32)
-    for h in range(2):
-        go = both(direct, jnp.logical_not(is_me(target(r, c, h))))
-        expected = expected + jnp.where(go, 1, 0).astype(i32)
+        for k in range(2):
+            mine = lax.rem(c + g + 1 - k, 2) == 0
+            straight = is_direct(k, *origin)
+
+            @pl.when(both(both(mine, straight), jnp.logical_not(is_me(origin))))
+            def _():
+                tell(origin)
+
+            @pl.when(both(mine, jnp.logical_not(straight)))
+            def _():
+                tell(relay(k, *origin))
+
+    def one(cond):
+        return jnp.where(cond, 1, 0).astype(i32)
+
+    expected = len(near) + one(is_root) + 3 * one(hub)
+    for k in range(2):
+        expected = expected + one(jnp.logical_not(both(direct[k], is_me(goal(k, r, c)))))
         for s in range(2):
-            go = both(relays_for[s], jnp.logical_not(is_me(target(*sources[s], h))))
-            expected = expected + jnp.where(go, 1, 0).astype(i32)
+            expected = expected + one(serves[k][s])
 
     cbuf[:, nnz] = jnp.zeros((ROWB, BLOCK, BLOCK), jnp.float32)
     pl.semaphore_wait(barrier, expected)
@@ -206,7 +236,7 @@
     for i in range(ROWB):
         row = ROWB * r + i
         slots = [
-            jnp.bitwise_and(cols[row, k] - row + nb // 2, nb - 1) - nb // 2 + REACH
+            jnp.bitwise_and(cols[k, row] - row + nb // 2, nb - 1) - nb // 2 + REACH
             for k in range(nnz)
         ]
         for o in range(BAND):
@@ -246,37 +276,31 @@
             device_id=dev, device_id_type=MESH,
         )
 
-    def deliver(src, rs, cs, h, j, ssem):
-        side = lax.rem(cs, 2)
-        dev = target(rs, cs, h)
-        mine = is_me(dev)
-
-        @pl.when(mine)
-        def _():
-            pltpu.make_async_copy(src, tbuf.at[side, j], trecv.at[side, j]).start()
-
-        @pl.when(jnp.logical_not(mine))
-        def _():
-            remote(src, tbuf.at[side, j], ssem, trecv.at[side, j], dev).start()
-
-    def drain(src, rs, cs, h, j, ssem):
-        side = lax.rem(cs, 2)
-        dev = target(rs, cs, h)
-
-        @pl.when(jnp.logical_not(is_me(dev)))
-        def _():
-            remote(src, tbuf.at[side, j], ssem, trecv.at[side, j], dev).wait_send()
-
-    my_slot = lax.rem(r // 2, 2)
-
-    def chunk(h):
-        return pl.ds(h * half, half)
-
-    def to_relay(h, j):
+    side = lax.rem(c, 2)
+
+    def deliver(src, dev, j, ssem):
+        return remote(src, tbuf.at[side, j], ssem, trecv.at[side, j], dev)
+
+    def mine_of(k, j):
+        return lbuf.at[j, pl.ds(part(k, c) * half, half)]
+
+    def straight(k, j):
+        return deliver(mine_of(k, j), goal(k, r, c), j, tsend.at[k, j])
+
+    def inside(k, j):
+        return pltpu.make_async_copy(mine_of(k, j), tbuf.at[side, j], trecv.at[side, j])
+
+    def to_relay(k, j):
+        slot = lax.rem(r // 2, 2) if k == 0 else lax.rem(r // 4, 2)
         return remote(
-            lbuf.at[j, chunk(h)], rbuf.at[my_slot, j, chunk(h)],
-            tsend.at[h, j], rrecv.at[my_slot, h, j], relay(r, c),
+            mine_of(k, j), rbuf.at[k, slot, j], tsend.at[k, j], rrecv.at[k, slot, j],
+            relay(k, r, c),
         )
+
+    def onward(k, s, j):
+        return deliver(rbuf.at[k, s, j], goal(k, *sources[k][s]), j, fsend.at[k, s, j])
+
+    at_home = [is_me(goal(k, r, c)) for k in range(2)]
 
     for j in range(COLB):
         for cp in halo[j]:
@@ -287,23 +311,26 @@
         q = jnp.dot(hs[pl.ds(0, tr)], elo[j], preferred_element_type=jnp.float32)
         lbuf[j] = p[:tr] + p[tr:] + q + dterm[j]
 
-        @pl.when(direct)
-        def _():
-            for h in range(2):
-                deliver(lbuf.at[j, chunk(h)], r, c, h, j, tsend.at[h, j])
-
-        @pl.when(jnp.logical_not(direct))
-        def _():
-            for h in range(2):
-                to_relay(h, j).start()
-
-        for s in range(2):
-            @pl.when(relays_for[s])
-            def _():
-                for h in range(2):
-                    src = rbuf.at[s, j, chunk(h)]
-                    pltpu.make_async_copy(src, src, rrecv.at[s, h, j]).wait()
-                    deliver(src, *sources[s], h, j, fsend.at[s, h, j])
+        for k in range(2):
+            @pl.when(at_home[k])
+            def _():
+                inside(k, j).start()
+
+            @pl.when(both(direct[k], jnp.logical_not(at_home[k])))
+            def _():
+                straight(k, j).start()
+
+            @pl.when(jnp.logical_not(direct[k]))
+            def _():
+                to_relay(k, j).start()
+
+        for k in range(2):
+            for s in range(2):
+                @pl.when(serves[k][s])
+                def _():
+                    src = rbuf.at[k, s, j]
+                    pltpu.make_async_copy(src, src, rrecv.at[k, s, j]).wait()
+                    onward(k, s, j).start()
 
     for j in range(COLB):
         for g in range(2):
@@ -323,19 +350,19 @@
     forwards(False, True)
     forwards(False, False)
     for j in range(COLB):
-        for h in range(2):
-            @pl.when(direct)
-            def _():
-                drain(lbuf.at[j, chunk(h)], r, c, h, j, tsend.at[h, j])
-
-            @pl.when(jnp.logical_not(direct))
-            def _():
-                to_relay(h, j).wait_send()
+        for k in range(2):
+            @pl.when(both(direct[k], jnp.logical_not(at_home[k])))
+            def _():
+                straight(k, j).wait_send()
+
+            @pl.when(jnp.logical_not(direct[k]))
+            def _():
+                to_relay(k, j).wait_send()
 
             for s in range(2):
-                @pl.when(relays_for[s])
+                @pl.when(serves[k][s])
                 def _():
-                    drain(rbuf.at[s, j, chunk(h)], *sources[s], h, j, fsend.at[s, h, j])
+                    onward(k, s, j).wait_send()
 
 
 def solution(mesh):
@@ -352,7 +379,7 @@
             in_specs=[pl.BlockSpec(memory_space=pl.ANY)] * 4,
             out_specs=pl.BlockSpec(memory_space=pltpu.VMEM),
             scratch_shapes=[
-                pltpu.SMEM((nb, nnz), jnp.int32),
+                pltpu.SMEM((nnz, nb), jnp.int32),
                 pltpu.SMEM((nb,), f32),
                 pltpu.VMEM((COLB, EXT * BLOCK, BLOCK), f32),
                 pltpu.VMEM((ROWB, nnz + 1, BLOCK, BLOCK), f32),
@@ -362,15 +389,15 @@
                 pltpu.VMEM((COLB, EXT * BLOCK, BLOCK), bf16),
                 pltpu.VMEM((2 * rows, EXT * BLOCK), bf16),
                 pltpu.VMEM((COLB, rows, BLOCK), f32),
-                pltpu.VMEM((2, COLB, rows, BLOCK), f32),
+                pltpu.VMEM((2, 2, COLB, 2 * BLOCK, BLOCK), f32),
                 pltpu.VMEM((2, COLB, 2 * BLOCK, BLOCK), f32),
                 dma((7,)), dma((COLB, 4)), dma((COLB, 4)), dma((5,)), dma(()),
                 dma((2, COLB)), dma((2, 2, COLB)), dma((2, 2, COLB)), dma((2, COLB)),
             ],
             compiler_params=pltpu.CompilerParams(
-                collective_id=0, has_side_effects=True, vmem_limit_bytes=48 * 2**20
+                collective_id=0, has_side_effects=True, vmem_limit_bytes=63 * 2**20
             ),
-        )(covariance, couplings, block_columns, onsite)
+        )(covariance, couplings, block_columns.T, onsite)
 
     return jax.shard_map(
         on_device,

time: 77 us -> 67.3 us (0.87)
  the two profiles are of different devices: /device:TPU:37 before, /device:TPU:20 now
where the time goes in v3:
time: 67.3 us; the launch traced here: 67.1 us
  Pallas kernels  65.2 us (97%)
  local copies, waits for them, and re-layouts  1.87 us (3%)
    pallas_call x1, Pallas kernels, on_device(): pl.pallas_call(functools.partial(kernel, nrow, nb, nnz), out_shape=jax.Sh...  65.2 us
    unnamed x1, local copies, waits for them, and re-layouts  1.87 us

profile of v3, /device:TPU:20, one launch (start us, length us, event | category | flops | bytes accessed | tf_op | source)
XLA Modules:
  0.0 67.1 jit_solution(18140936281819414000)
XLA Ops:
  0.0 65.2 %shard_map.46 = f32[512,256]{1,0:T(8,128)} custom-call(f32[512,256]{1,0:T(8,128)} %cov.1, f32[4,9,128,128]{3,2,1,0:T(8,128)} %coup.1, s32[9,64]{1,0:T(8,128)} %bitcast.1, f32[64]{0:T(128)} %onsite_h.1), custom_call_target="tpu_custom_call" | custom-call | tf_op jit(solution)/shard_map/pallas_call | solution.py:376
  65.2 1.9 %copy.6 = f32[512,256]{1,0:T(8,128)} copy(f32[512,256]{1,0:T(8,128)} %shard_map.46) | data formatting | bytes 1048576

commit v4 on v3

--- a/solution.py
+++ b/solution.py
@@ -26,8 +26,8 @@
 def kernel(
     nrow, nb, nnz,
     cov, coup, cols_h, onsite_h, out,
-    cols, onsite, ext, cbuf, dbuf, dterm, ehi, elo, hs, lbuf, rbuf, tbuf,
-    load_sem, hsend, hrecv, dsend, drecv, tsend, fsend, rrecv, trecv,
+    cols, onsite, ext, cbuf, dbuf, dterm, ehi, elo, hs, lbuf, rbuf, sbuf, tbuf,
+    load_sem, hsend, hrecv, csend, csrecv, ssend, dsend, drecv, tsend, fsend, rrecv, trecv, token,
 ):
     r = lax.axis_index("row")
     c = lax.axis_index("col")
@@ -91,7 +91,23 @@
         )
         for j in range(COLB)
     ]
-    for cp in loads:
+    root = c // 2
+    is_root = r == root
+    first_diag = 2 * lax.rem(c, 2) * BLOCK
+    diag_loads = [
+        pltpu.make_async_copy(
+            cov.at[pl.ds(first_diag + b * BLOCK, BLOCK), pl.ds(b * BLOCK, BLOCK)],
+            dbuf.at[b], load_sem.at[5 + b],
+        )
+        for b in range(COLB)
+    ]
+
+    @pl.when(is_root)
+    def _():
+        for cp in diag_loads:
+            cp.start()
+
+    for cp in loads[1:] + loads[:1]:
         cp.start()
 
     barrier = pltpu.get_barrier_semaphore()
@@ -100,10 +116,8 @@
         pl.semaphore_signal(barrier, inc=1, device_id=dev, device_id_type=MESH)
 
     near = [rowdev(d) for d in (-2, -1, 1, 2)]
-    root = c // 2
     same_core = lax.rem(r, 2) == lax.rem(root, 2)
     same_x = lax.rem(r // 2, 4) == lax.rem(root // 2, 4)
-    is_root = r == root
     hub = both(same_core, same_x)
     leaf = both(same_core, jnp.logical_not(same_x))
     peer = (lax.rem(r + 8, nrow), c)
@@ -138,10 +152,36 @@
             def _():
                 tell(relay(k, *origin))
 
+    place = lax.rem(r, 8)
+    seam_up = place == 7
+    seam_down = place == 0
+    via_up = place == 5
+    via_down = place == 2
+
+    @pl.when(seam_down)
+    def _():
+        tell(rowdev(-3))
+
+    @pl.when(seam_up)
+    def _():
+        tell(rowdev(3))
+
+    low, high = r // 8 == 0, r // 8 == 1
+    x_low = lax.rem(r // 4, 2) == 0
+    x_high = jnp.logical_not(x_low)
+    gives = jnp.logical_or(both(both(low, yy == 3), x_low), both(both(high, yy == 0), x_high))
+    takes = jnp.logical_or(both(both(low, yy == 2), x_low), both(both(high, yy == 1), x_high))
+    giver = (r, c + ZN - 2 * ZN * (r // 8))
+    taker = (r, c - ZN + 2 * ZN * (r // 8))
+
+    @pl.when(takes)
+    def _():
+        tell(giver)
+
     def one(cond):
         return jnp.where(cond, 1, 0).astype(i32)
 
-    expected = len(near) + one(is_root) + 3 * one(hub)
+    expected = len(near) + one(is_root) + 3 * one(hub) + one(via_up) + one(via_down) + one(gives)
     for k in range(2):
         expected = expected + one(jnp.logical_not(both(direct[k], is_me(goal(k, r, c)))))
         for s in range(2):
@@ -150,24 +190,69 @@
     cbuf[:, nnz] = jnp.zeros((ROWB, BLOCK, BLOCK), jnp.float32)
     pl.semaphore_wait(barrier, expected)
 
+    even = lax.rem(r, 2) == 0
+    top = (REACH + ROWB) * BLOCK
+
+    def remote(src, dst, ssem, rsem, dev):
+        return pltpu.make_async_remote_copy(
+            src_ref=src, dst_ref=dst, send_sem=ssem, recv_sem=rsem,
+            device_id=dev, device_id_type=MESH,
+        )
+
+    def own_rows(j, start, size):
+        return cov.at[pl.ds(start, size), pl.ds(j * BLOCK, BLOCK)]
+
     plan = [
-        (1, 0, tr, BLOCK),
-        (-1, 0, tr, (REACH + ROWB) * BLOCK),
+        (1, half, half, BLOCK + half),
+        (-1, half, half, top + half),
+        (1, 0, half, BLOCK),
+        (-1, 0, half, top),
         (2, tr - BLOCK, BLOCK, 0),
-        (-2, 0, BLOCK, (EXT - 1) * BLOCK),
+        (-2, 0, BLOCK, top + tr),
     ]
-    halo = [
-        [
-            pltpu.make_async_remote_copy(
-                src_ref=cov.at[pl.ds(start, size), pl.ds(j * BLOCK, BLOCK)],
-                dst_ref=ext.at[j, pl.ds(dst, size)],
-                send_sem=hsend.at[j, n], recv_sem=hrecv.at[j, n],
-                device_id=rowdev(d), device_id_type=MESH,
-            )
-            for n, (d, start, size, dst) in enumerate(plan)
-        ]
-        for j in range(COLB)
-    ]
+    odd = jnp.logical_not(even)
+    who = [[None] * 4 + [even, odd] for j in range(COLB - 1)]
+    who.append([jnp.logical_not(seam_up), jnp.logical_not(seam_down)] * 2 + [even, odd])
+
+    def halo(j, n):
+        d, start, size, dst = plan[n]
+        return remote(
+            own_rows(j, start, size), ext.at[j, pl.ds(dst, size)],
+            hsend.at[j, n], hrecv.at[j, n], rowdev(d),
+        )
+
+    last = COLB - 1
+
+    def detour(u, up):
+        n = 2 * u + (0 if up else 1)
+        return remote(
+            own_rows(last, plan[n][1], half), sbuf.at[u],
+            hsend.at[last, n], csrecv.at[u], rowdev(-2 if up else 2),
+        )
+
+    def detour_on(u, up):
+        n = 2 * u + (0 if up else 1)
+        return remote(
+            sbuf.at[u], ext.at[last, pl.ds(plan[n][3], half)],
+            ssend.at[u], hrecv.at[last, n], rowdev(3 if up else -3),
+        )
+
+    def share(j, up):
+        src, dst, n = (4 * BLOCK, 0, 4) if up else (top, top + tr, 5)
+        return remote(
+            ext.at[j, pl.ds(src, BLOCK)], ext.at[j, pl.ds(dst, BLOCK)],
+            csend.at[j], hrecv.at[j, n], pair,
+        )
+
+    def when(cond, act):
+        if cond is None:
+            act()
+        else:
+            pl.when(cond)(act)
+
+    def halo_wait(j, n):
+        dst = ext.at[j, pl.ds(plan[n][3], plan[n][2])]
+        pltpu.make_async_copy(dst, dst, hrecv.at[j, n]).wait()
 
     def fan(devs, first):
         return [
@@ -194,27 +279,43 @@
         forward(both(hub, at), xdevs, 1, start)
         forward(both(same_core, at), [pair], 0, start)
 
-    first_diag = 2 * lax.rem(c, 2) * BLOCK
-
     @pl.when(is_root)
     def _():
-        copies = [
-            pltpu.make_async_copy(
-                cov.at[pl.ds(first_diag + b * BLOCK, BLOCK), pl.ds(b * BLOCK, BLOCK)],
-                dbuf.at[b], load_sem.at[5 + b],
-            )
-            for b in range(2)
-        ]
-        for cp in copies:
+        for cp in diag_loads:
+            cp.wait()
+        fan([peer], 4)[0].start()
+
+    for u in range(2):
+        when(seam_up, lambda: detour(u, True).start())
+        when(seam_down, lambda: detour(u, False).start())
+    for n in range(len(plan)):
+        when(who[0][n], lambda: halo(0, n).start())
+
+    @pl.when(both(hub, jnp.logical_not(is_root)))
+    def _():
+        fan([pair], 0)[0].wait_recv()
+
+    @pl.when(hub)
+    def _():
+        for cp in fan(xdevs, 1) + fan([pair], 0):
             cp.start()
-        for cp in copies:
-            cp.wait()
-
-    forwards(True, True)
-
-    for j in range(COLB):
-        for cp in halo[j]:
-            cp.start()
+
+    for n in range(len(plan)):
+        when(who[1][n], lambda: halo(1, n).start())
+
+    @pl.when(leaf)
+    def _():
+        fan([pair], 0)[0].wait_recv()
+        fan([pair], 0)[0].start()
+
+    for u in range(2):
+        def act(up):
+            src = sbuf.at[u]
+            pltpu.make_async_copy(src, src, csrecv.at[u]).wait()
+            detour_on(u, up).start()
+
+        when(via_up, lambda: act(True))
+        when(via_down, lambda: act(False))
 
     for cp in loads:
         cp.wait()
@@ -253,11 +354,9 @@
     for j in range(COLB):
         put_e(j, REACH * BLOCK, tr)
 
-    @pl.when(jnp.logical_not(is_root))
+    @pl.when(jnp.logical_not(same_core))
     def _():
         fan([pair], 0)[0].wait_recv()
-
-    forwards(True, False)
 
     def dot_t(a, b):
         return lax.dot_general(
@@ -270,12 +369,6 @@
         yhi = ehi[j, mid]
         dterm[j] = dot_t(yhi, dhi) + dot_t(yhi, dlo) + dot_t(elo[j, mid], dhi)
 
-    def remote(src, dst, ssem, rsem, dev):
-        return pltpu.make_async_remote_copy(
-            src_ref=src, dst_ref=dst, send_sem=ssem, recv_sem=rsem,
-            device_id=dev, device_id_type=MESH,
-        )
-
     side = lax.rem(c, 2)
 
     def deliver(src, dev, j, ssem):
@@ -303,8 +396,23 @@
     at_home = [is_me(goal(k, r, c)) for k in range(2)]
 
     for j in range(COLB):
-        for cp in halo[j]:
-            cp.wait_recv()
+        @pl.when(even)
+        def _():
+            halo_wait(j, 0)
+            share(j, True).start()
+
+        @pl.when(jnp.logical_not(even))
+        def _():
+            halo_wait(j, 3)
+            share(j, False).start()
+
+        for n in range(len(plan)):
+            if n == 0:
+                when(jnp.logical_not(even), lambda: halo_wait(j, n))
+            elif n == 3:
+                when(even, lambda: halo_wait(j, n))
+            else:
+                halo_wait(j, n)
         put_e(j, 0, REACH * BLOCK)
         put_e(j, (REACH + ROWB) * BLOCK, REACH * BLOCK)
         p = jnp.dot(hs[...], ehi[j], preferred_element_type=jnp.float32)
@@ -324,13 +432,30 @@
             def _():
                 to_relay(k, j).start()
 
-        for k in range(2):
-            for s in range(2):
-                @pl.when(serves[k][s])
-                def _():
-                    src = rbuf.at[k, s, j]
-                    pltpu.make_async_copy(src, src, rrecv.at[k, s, j]).wait()
-                    onward(k, s, j).start()
+    def forward_on(k, j):
+        for s in range(2):
+            @pl.when(serves[k][s])
+            def _():
+                src = rbuf.at[k, s, j]
+                pltpu.make_async_copy(src, src, rrecv.at[k, s, j]).wait()
+                onward(k, s, j).start()
+
+    forward_on(0, 0)
+
+    @pl.when(gives)
+    def _():
+        for j in range(COLB):
+            to_relay(0, j).wait_send()
+        pl.semaphore_signal(token, inc=1, device_id=taker, device_id_type=MESH)
+
+    forward_on(0, 1)
+
+    @pl.when(takes)
+    def _():
+        pl.semaphore_wait(token, 1)
+
+    forward_on(1, 0)
+    forward_on(1, 1)
 
     for j in range(COLB):
         for g in range(2):
@@ -345,8 +470,15 @@
                 out[rows, lanes] = ext[b, here] + STEP * mine
 
     for j in range(COLB):
-        for cp in halo[j]:
-            cp.wait_send()
+        for n in range(len(plan)):
+            when(who[j][n], lambda: halo(j, n).wait_send())
+        when(even, lambda: share(j, True).wait_send())
+        when(jnp.logical_not(even), lambda: share(j, False).wait_send())
+    for u in range(2):
+        when(seam_up, lambda: detour(u, True).wait_send())
+        when(seam_down, lambda: detour(u, False).wait_send())
+        when(via_up, lambda: detour_on(u, True).wait_send())
+        when(via_down, lambda: detour_on(u, False).wait_send())
     forwards(False, True)
     forwards(False, False)
     for j in range(COLB):
@@ -355,7 +487,11 @@
             def _():
                 straight(k, j).wait_send()
 
-            @pl.when(jnp.logical_not(direct[k]))
+            left = jnp.logical_not(direct[k])
+            if k == 0:
+                left = both(left, jnp.logical_not(gives))
+
+            @pl.when(left)
             def _():
                 to_relay(k, j).wait_send()
 
@@ -390,9 +526,12 @@
                 pltpu.VMEM((2 * rows, EXT * BLOCK), bf16),
                 pltpu.VMEM((COLB, rows, BLOCK), f32),
                 pltpu.VMEM((2, 2, COLB, 2 * BLOCK, BLOCK), f32),
+                pltpu.VMEM((COLB, 2 * BLOCK, BLOCK), f32),
                 pltpu.VMEM((2, COLB, 2 * BLOCK, BLOCK), f32),
-                dma((7,)), dma((COLB, 4)), dma((COLB, 4)), dma((5,)), dma(()),
+                dma((7,)), dma((COLB, 6)), dma((COLB, 6)), dma((COLB,)), dma((2,)), dma((2,)),
+                dma((5,)), dma(()),
                 dma((2, COLB)), dma((2, 2, COLB)), dma((2, 2, COLB)), dma((2, COLB)),
+                pltpu.SemaphoreType.REGULAR,
             ],
             compiler_params=pltpu.CompilerParams(
                 collective_id=0, has_side_effects=True, vmem_limit_bytes=63 * 2**20

time: 67.3 us -> 62.7 us (0.932)
  the two profiles are of different devices: /device:TPU:20 before, /device:TPU:52 now
where the time goes in v4:
time: 62.7 us; the launch traced here: 62.5 us
  Pallas kernels  60.6 us (97%)
  local copies, waits for them, and re-layouts  1.87 us (3%)
    pallas_call x1, Pallas kernels, on_device(): pl.pallas_call(functools.partial(kernel, nrow, nb, nnz), out_shape=jax.Sh...  60.6 us
    unnamed x1, local copies, waits for them, and re-layouts  1.87 us

profile of v4, /device:TPU:52, one launch (start us, length us, event | category | flops | bytes accessed | tf_op | source)
XLA Modules:
  0.0 62.5 jit_solution(2982903772124917068)
XLA Ops:
  0.0 60.6 %shard_map.46 = f32[512,256]{1,0:T(8,128)} custom-call(f32[512,256]{1,0:T(8,128)} %cov.1, f32[4,9,128,128]{3,2,1,0:T(8,128)} %coup.1, s32[9,64]{1,0:T(8,128)} %bitcast.1, f32[64]{0:T(128)} %onsite_h.1), custom_call_target="tpu_custom_call" | custom-call | tf_op jit(solution)/shard_map/pallas_call | solution.py:512
  60.6 1.9 %copy.6 = f32[512,256]{1,0:T(8,128)} copy(f32[512,256]{1,0:T(8,128)} %shard_map.46) | data formatting | bytes 1048576

commit v5 on v4

--- a/solution.py
+++ b/solution.py
@@ -26,7 +26,7 @@
 def kernel(
     nrow, nb, nnz,
     cov, coup, cols_h, onsite_h, out,
-    cols, onsite, ext, cbuf, dbuf, dterm, ehi, elo, hs, lbuf, rbuf, sbuf, tbuf,
+    cols, onsite, ext, cbuf, dbuf, pbuf, dterm, ehi, elo, hs, lbuf, rbuf, sbuf, tbuf,
     load_sem, hsend, hrecv, csend, csrecv, ssend, dsend, drecv, tsend, fsend, rrecv, trecv, token,
 ):
     r = lax.axis_index("row")
@@ -187,6 +187,25 @@
         for s in range(2):
             expected = expected + one(serves[k][s])
 
+    hb = BLOCK // 2
+    row_of = lax.broadcasted_iota(i32, (hb, BLOCK), 0)
+    lane_of = lax.broadcasted_iota(i32, (hb, BLOCK), 1)
+
+    def pack(d):
+        return jnp.where(lane_of < row_of, pltpu.roll(d[hb:], hb, 1), d[:hb])
+
+    def unpack(p):
+        zero = jnp.zeros_like(p)
+        lower = pltpu.roll(jnp.where(lane_of < row_of, p, zero), hb, 1)
+        x = jnp.concatenate([jnp.where(lane_of > row_of, p, zero), lower], axis=0)
+        return x - x.T
+
+    @pl.when(is_root)
+    def _():
+        for b, cp in enumerate(diag_loads):
+            cp.wait()
+            pbuf[b] = pack(dbuf[b])
+
     cbuf[:, nnz] = jnp.zeros((ROWB, BLOCK, BLOCK), jnp.float32)
     pl.semaphore_wait(barrier, expected)
 
@@ -257,7 +276,7 @@
     def fan(devs, first):
         return [
             pltpu.make_async_remote_copy(
-                src_ref=dbuf, dst_ref=dbuf, send_sem=dsend.at[first + k], recv_sem=drecv,
+                src_ref=pbuf, dst_ref=pbuf, send_sem=dsend.at[first + k], recv_sem=drecv,
                 device_id=dev, device_id_type=MESH,
             )
             for k, dev in enumerate(devs)
@@ -281,8 +300,6 @@
 
     @pl.when(is_root)
     def _():
-        for cp in diag_loads:
-            cp.wait()
         fan([peer], 4)[0].start()
 
     for u in range(2):
@@ -365,7 +382,7 @@
 
     mid = pl.ds(REACH * BLOCK, tr)
     for j in range(COLB):
-        dhi, dlo = split(onsite[COLB * c + j] * dbuf[j])
+        dhi, dlo = split(onsite[COLB * c + j] * unpack(pbuf[j]))
         yhi = ehi[j, mid]
         dterm[j] = dot_t(yhi, dhi) + dot_t(yhi, dlo) + dot_t(elo[j, mid], dhi)
 
@@ -395,29 +412,54 @@
 
     at_home = [is_me(goal(k, r, c)) for k in range(2)]
 
+    def product(j, start, size):
+        at = pl.ds(pl.multiple_of(start, BLOCK), size)
+        high = ehi[j, at]
+        p = jnp.dot(hs[:, at], high, preferred_element_type=jnp.float32)
+        q = jnp.dot(hs[pl.ds(0, tr), at], elo[j, at], preferred_element_type=jnp.float32)
+        return p[:tr] + p[tr:] + q
+
+    def by_core(a, b):
+        return jnp.where(even, a, b).astype(i32)
+
+    for j in range(COLB):
+        @pl.when(even)
+        def _():
+            halo_wait(j, 1)
+            halo_wait(j, 3)
+            put_e(j, top, tr)
+
+        @pl.when(odd)
+        def _():
+            halo_wait(j, 0)
+            halo_wait(j, 2)
+            put_e(j, BLOCK, tr)
+
+        dterm[j] = dterm[j] + product(j, by_core(REACH * BLOCK, BLOCK), 2 * tr)
+
     for j in range(COLB):
         @pl.when(even)
         def _():
             halo_wait(j, 0)
             share(j, True).start()
-
-        @pl.when(jnp.logical_not(even))
+            halo_wait(j, 2)
+            halo_wait(j, 4)
+            put_e(j, 0, REACH * BLOCK)
+            halo_wait(j, 5)
+            put_e(j, top + tr, BLOCK)
+
+        @pl.when(odd)
         def _():
             halo_wait(j, 3)
             share(j, False).start()
-
-        for n in range(len(plan)):
-            if n == 0:
-                when(jnp.logical_not(even), lambda: halo_wait(j, n))
-            elif n == 3:
-                when(even, lambda: halo_wait(j, n))
-            else:
-                halo_wait(j, n)
-        put_e(j, 0, REACH * BLOCK)
-        put_e(j, (REACH + ROWB) * BLOCK, REACH * BLOCK)
-        p = jnp.dot(hs[...], ehi[j], preferred_element_type=jnp.float32)
-        q = jnp.dot(hs[pl.ds(0, tr)], elo[j], preferred_element_type=jnp.float32)
-        lbuf[j] = p[:tr] + p[tr:] + q + dterm[j]
+            halo_wait(j, 1)
+            halo_wait(j, 5)
+            put_e(j, top, REACH * BLOCK)
+            halo_wait(j, 4)
+            put_e(j, 0, BLOCK)
+
+        far = product(j, by_core(0, top), REACH * BLOCK)
+        lbuf[j] = dterm[j] + far + product(j, by_core(top + tr, 0), BLOCK)
 
         for k in range(2):
             @pl.when(at_home[k])
@@ -448,13 +490,17 @@
             to_relay(0, j).wait_send()
         pl.semaphore_signal(token, inc=1, device_id=taker, device_id_type=MESH)
 
-    forward_on(0, 1)
-
     @pl.when(takes)
     def _():
+        forward_on(0, 1)
         pl.semaphore_wait(token, 1)
-
-    forward_on(1, 0)
+        forward_on(1, 0)
+
+    @pl.when(jnp.logical_not(takes))
+    def _():
+        forward_on(1, 0)
+        forward_on(0, 1)
+
     forward_on(1, 1)
 
     for j in range(COLB):
@@ -520,6 +566,7 @@
                 pltpu.VMEM((COLB, EXT * BLOCK, BLOCK), f32),
                 pltpu.VMEM((ROWB, nnz + 1, BLOCK, BLOCK), f32),
                 pltpu.VMEM((COLB, BLOCK, BLOCK), f32),
+                pltpu.VMEM((COLB, BLOCK // 2, BLOCK), f32),
                 pltpu.VMEM((COLB, rows, BLOCK), f32),
                 pltpu.VMEM((COLB, EXT * BLOCK, BLOCK), bf16),
                 pltpu.VMEM((COLB, EXT * BLOCK, BLOCK), bf16),

time: 62.7 us -> 59.8 us (0.954)
  the two profiles are of different devices: /device:TPU:52 before, /device:TPU:22 now
where the time goes in v5:
time: 59.8 us; the launch traced here: 59.7 us
  Pallas kernels  57.8 us (97%)
  local copies, waits for them, and re-layouts  1.87 us (3%)
    pallas_call x1, Pallas kernels, on_device(): pl.pallas_call(functools.partial(kernel, nrow, nb, nnz), out_shape=jax.Sh...  57.8 us
    unnamed x1, local copies, waits for them, and re-layouts  1.87 us

profile of v5, /device:TPU:22, one launch (start us, length us, event | category | flops | bytes accessed | tf_op | source)
XLA Modules:
  0.0 59.7 jit_solution(10856147136343384129)
XLA Ops:
  0.0 57.8 %shard_map.46 = f32[512,256]{1,0:T(8,128)} custom-call(f32[512,256]{1,0:T(8,128)} %cov.1, f32[4,9,128,128]{3,2,1,0:T(8,128)} %coup.1, s32[9,64]{1,0:T(8,128)} %bitcast.1, f32[64]{0:T(128)} %onsite_h.1), custom_call_target="tpu_custom_call" | custom-call | tf_op jit(solution)/shard_map/pallas_call | solution.py:558
  57.8 1.9 %copy.6 = f32[512,256]{1,0:T(8,128)} copy(f32[512,256]{1,0:T(8,128)} %shard_map.46) | data formatting | bytes 1048576

commit v6 on v5

--- a/solution.py
+++ b/solution.py
@@ -27,7 +27,7 @@
     nrow, nb, nnz,
     cov, coup, cols_h, onsite_h, out,
     cols, onsite, ext, cbuf, dbuf, pbuf, dterm, ehi, elo, hs, lbuf, rbuf, sbuf, tbuf,
-    load_sem, hsend, hrecv, csend, csrecv, ssend, dsend, drecv, tsend, fsend, rrecv, trecv, token,
+    load_sem, hsend, hrecv, csend, csrecv, ssend, dsend, drecv, tsend, fsend, rrecv, trecv, token, fbuf, frecv, osend,
 ):
     r = lax.axis_index("row")
     c = lax.axis_index("col")
@@ -69,10 +69,28 @@
         via = relay(k, rs, cs)
         return jnp.logical_or(same(via, (rs, cs)), same(via, goal(k, rs, cs)))
 
+    def served(rr, cc, s):
+        row = (rr // 8) * 8 + 4 * s + lax.rem(cc, ZN) // 2
+        return row, (cc // ZN) * ZN + lax.rem(rr, 4) * 2 + lax.rem(cc, 2)
+
+    def crosses(rr, cc):
+        return both(rr // 8 != cc // 16, lax.rem(rr // 4, 2) == rr // 8)
+
+    def around(rr, cc):
+        return lax.rem(rr + 8, nrow), 24 - 24 * (rr // 8) + lax.rem(cc, ZN)
+
+    mid = crosses(r, c)
+    mid_source = (lax.rem(r + 8, nrow), (lax.rem(r // 4, 2) + 2 * (r // 8)) * ZN + zz)
+    far_sources = [served(*mid_source, s) for s in range(2)]
+    far_serves = [
+        both(both(yy == 3 * (r // 8), crosses(*mid_source)), jnp.logical_not(is_direct(1, *far_sources[s])))
+        for s in range(2)
+    ]
+
     direct = [is_direct(k, r, c) for k in range(2)]
     sources = [
         [((c // 8) * 4 + 2 * s + lax.rem(r, 2), (r // 4) * ZN + zz) for s in range(2)],
-        [((r // 8) * 8 + 4 * s + zz // 2, yy * ZN + lax.rem(r, 4) * 2 + lax.rem(c, 2)) for s in range(2)],
+        [served(r, c, s) for s in range(2)],
     ]
     at_relay = [lax.rem(r // 2, 2) == zz // 4, lax.rem(r // 4, 2) == lax.rem(yy, 2)]
     serves = [
@@ -152,6 +170,16 @@
             def _():
                 tell(relay(k, *origin))
 
+            if k == 1:
+                @pl.when(both(both(mine, jnp.logical_not(straight)), crosses(*relay(k, *origin))))
+                def _():
+                    tell(around(*relay(k, *origin)))
+
+    for s in range(2):
+        @pl.when(far_serves[s])
+        def _():
+            tell(mid_source)
+
     place = lax.rem(r, 8)
     seam_up = place == 7
     seam_down = place == 0
@@ -186,6 +214,8 @@
         expected = expected + one(jnp.logical_not(both(direct[k], is_me(goal(k, r, c)))))
         for s in range(2):
             expected = expected + one(serves[k][s])
+    for s in range(2):
+        expected = expected + one(both(mid, serves[1][s])) + one(far_serves[s])
 
     hb = BLOCK // 2
     row_of = lax.broadcasted_iota(i32, (hb, BLOCK), 0)
@@ -380,11 +410,11 @@
             a, b, (((1,), (1,)), ((), ())), preferred_element_type=jnp.float32
         )
 
-    mid = pl.ds(REACH * BLOCK, tr)
+    own_at = pl.ds(REACH * BLOCK, tr)
     for j in range(COLB):
         dhi, dlo = split(onsite[COLB * c + j] * unpack(pbuf[j]))
-        yhi = ehi[j, mid]
-        dterm[j] = dot_t(yhi, dhi) + dot_t(yhi, dlo) + dot_t(elo[j, mid], dhi)
+        yhi = ehi[j, own_at]
+        dterm[j] = dot_t(yhi, dhi) + dot_t(yhi, dlo) + dot_t(elo[j, own_at], dhi)
 
     side = lax.rem(c, 2)
 
@@ -409,6 +439,21 @@
 
     def onward(k, s, j):
         return deliver(rbuf.at[k, s, j], goal(k, *sources[k][s]), j, fsend.at[k, s, j])
+
+    def to_far(s):
+        return remote(
+            rbuf.at[1, s, 0], fbuf.at[s], fsend.at[1, s, 0], frecv.at[s], around(r, c)
+        )
+
+    def from_far(s):
+        return deliver(fbuf.at[s], goal(1, *far_sources[s]), 0, osend.at[s])
+
+    def passing(k, s, j, act):
+        if (k, j) == (1, 0):
+            when(mid, lambda: act(to_far(s)))
+            when(jnp.logical_not(mid), lambda: act(onward(k, s, j)))
+        else:
+            act(onward(k, s, j))
 
     at_home = [is_me(goal(k, r, c)) for k in range(2)]
 
@@ -480,7 +525,7 @@
             def _():
                 src = rbuf.at[k, s, j]
                 pltpu.make_async_copy(src, src, rrecv.at[k, s, j]).wait()
-                onward(k, s, j).start()
+                passing(k, s, j, lambda cp: cp.start())
 
     forward_on(0, 0)
 
@@ -490,18 +535,21 @@
             to_relay(0, j).wait_send()
         pl.semaphore_signal(token, inc=1, device_id=taker, device_id_type=MESH)
 
+    forward_on(1, 0)
+    forward_on(0, 1)
+
     @pl.when(takes)
     def _():
-        forward_on(0, 1)
         pl.semaphore_wait(token, 1)
-        forward_on(1, 0)
-
-    @pl.when(jnp.logical_not(takes))
-    def _():
-        forward_on(1, 0)
-        forward_on(0, 1)
 
     forward_on(1, 1)
+
+    for s in range(2):
+        @pl.when(far_serves[s])
+        def _():
+            src = fbuf.at[s]
+            pltpu.make_async_copy(src, src, frecv.at[s]).wait()
+            from_far(s).start()
 
     for j in range(COLB):
         for g in range(2):
@@ -525,6 +573,8 @@
         when(seam_down, lambda: detour(u, False).wait_send())
         when(via_up, lambda: detour_on(u, True).wait_send())
         when(via_down, lambda: detour_on(u, False).wait_send())
+    for s in range(2):
+        when(far_serves[s], lambda: from_far(s).wait_send())
     forwards(False, True)
     forwards(False, False)
     for j in range(COLB):
@@ -544,7 +594,7 @@
             for s in range(2):
                 @pl.when(serves[k][s])
                 def _():
-                    onward(k, s, j).wait_send()
+                    passing(k, s, j, lambda cp: cp.wait_send())
 
 
 def solution(mesh):
@@ -579,6 +629,7 @@
                 dma((5,)), dma(()),
                 dma((2, COLB)), dma((2, 2, COLB)), dma((2, 2, COLB)), dma((2, COLB)),
                 pltpu.SemaphoreType.REGULAR,
+                pltpu.VMEM((2, 2 * BLOCK, BLOCK), f32), dma((2,)), dma((2,)),
             ],
             compiler_params=pltpu.CompilerParams(
                 collective_id=0, has_side_effects=True, vmem_limit_bytes=63 * 2**20

time: 59.8 us -> 60 us (level)
  no operation moved by 1% of the time
where the time goes in v6:
time: 60 us; the launch traced here: 59.8 us
  Pallas kernels  57.9 us (96%)
  local copies, waits for them, and re-layouts  1.87 us (3%)
    pallas_call x1, Pallas kernels, on_device(): pl.pallas_call(functools.partial(kernel, nrow, nb, nnz), out_shape=jax.Sh...  57.9 us
    unnamed x1, local copies, waits for them, and re-layouts  1.87 us

profile of v6, /device:TPU:22, one launch (start us, length us, event | category | flops | bytes accessed | tf_op | source)
XLA Modules:
  0.0 59.8 jit_solution(11636563792576926710)
XLA Ops:
  0.0 57.9 %shard_map.46 = f32[512,256]{1,0:T(8,128)} custom-call(f32[512,256]{1,0:T(8,128)} %cov.1, f32[4,9,128,128]{3,2,1,0:T(8,128)} %coup.1, s32[9,64]{1,0:T(8,128)} %bitcast.1, f32[64]{0:T(128)} %onsite_h.1), custom_call_target="tpu_custom_call" | custom-call | tf_op jit(solution)/shard_map/pallas_call | solution.py:608
  57.9 1.9 %copy.6 = f32[512,256]{1,0:T(8,128)} copy(f32[512,256]{1,0:T(8,128)} %shard_map.46) | data formatting | bytes 1048576
